TPU v7x, 128 devices: a whole 4x4x4 slice. The times are simulated.
128 devices in a mesh: img: 16 (over z, x), pen: 8 (over y, core).
Axes of the slice: x: 4, y: 4, z: 4, core: 2. Of those that a mesh axis runs over, the one named last changes fastest.
Arguments:
- slice_tiles: bfloat16 [8192, 128, 256], P(('img', 'pen')), may hold values from -192 to 192
- ctf_tiles: bfloat16 [8192, 128, 128], P(('img', 'pen')), may hold values from 0.25 to 16
- entry_tile: int32 [16384], P(('img', 'pen')), may hold values from 0 to 63
- entry_brick: int32 [16384, 1], P(('img', 'pen')), may hold values from 0 to 127; in each aligned block of 128 rows (0 to 127, 128 to 255, ...) at most 2 rows name the same one
- entry_kernel: int32 [16384], P(('img', 'pen')), may hold values from 0 to 15
- ky_bank: bfloat16 [16, 48, 128], replicated, may hold values from 0 to 1
- kx_bank: bfloat16 [16, 128, 384], replicated, may hold values from 0 to 1
- z_bank: bfloat16 [16, 128], replicated, may hold values from 0.099609375 to 1
Outputs:
- volume: float32 [768, 768, 128], P('pen', 'img')
Inputs may be any that keep to these rules, and one draw needn't show every extreme that they name: `entry_brick`: within the rows of one device no brick is named more than 2 times, a bound that some block reaches. `entry_tile`: an index among the 64 tiles of the entry's own device.
All inputs are finite; a program needn't handle non-finite values.
Results may differ from a plain program's by a relative error of at most 0.0041.
Values may be sent and summed in bfloat16 or wider, within the bound.
A program may use at most 192 MiB of HBM per device.

v0:
```python
import math

import jax
import jax.numpy as jnp
from jax import lax
from jax.experimental import pallas as pl
from jax.sharding import PartitionSpec as P

NBOX = 768
KXH = 384
PIX = 128
NK = 16
CAP = 2
ZW = 128


def angle_table(left_idx, right_idx):
    product = left_idx[:, None] * right_idx[None, :] % NBOX
    return 2.0 * math.pi / NBOX * product.astype(jnp.float32)


def kx_kernel(h_ref, w_ref, o_ref):
    @pl.when(pl.program_id(0) == 0)
    def _():
        o_ref[...] = jnp.zeros(o_ref.shape, o_ref.dtype)

    pix = w_ref.shape[1]
    h = jnp.concatenate(
        [h_ref[:, m * pix:(m + 1) * pix] for m in range(h_ref.shape[1] // pix)], axis=0
    )
    hi = h.astype(jnp.bfloat16)
    lo = (h - hi.astype(jnp.float32)).astype(jnp.bfloat16)
    w = w_ref[0]
    o_ref[...] += jnp.dot(hi, w, preferred_element_type=jnp.float32) + jnp.dot(
        lo, w, preferred_element_type=jnp.float32
    )


def apply_kx(per_kernel, kx_bank):
    kernels, pix, cols = kx_bank.shape
    planes = per_kernel.shape[0] // kernels
    width = per_kernel.shape[1]
    rows = planes * width // pix
    return pl.pallas_call(
        kx_kernel,
        grid=(kernels,),
        in_specs=[
            pl.BlockSpec((planes, width), lambda k: (k, 0)),
            pl.BlockSpec((1, pix, cols), lambda k: (k, 0, 0)),
        ],
        out_specs=pl.BlockSpec((rows, cols), lambda k: (0, 0)),
        out_shape=jax.ShapeDtypeStruct((rows, cols), jnp.float32),
    )(per_kernel, kx_bank)

def local(slice_tiles, ctf_tiles, entry_tile, entry_brick, entry_kernel, ky_bank, kx_bank, z_bank):
    img_count = lax.axis_size("img")
    pen_count = lax.axis_size("pen")
    bricks = img_count * pen_count
    entry_count = entry_tile.shape[0]
    rows_brick = ky_bank.shape[1]
    window = z_bank.shape[1]
    planes = window // pen_count
    slot_total = bricks * CAP
    target = entry_brick[:, 0]
    positions = jnp.arange(entry_count, dtype=jnp.int32)
    earlier = (target[None, :] == target[:, None]) & (positions[None, :] < positions[:, None])
    slot_rank = jnp.sum(earlier.astype(jnp.int32), axis=1)
    slot_index = target * CAP + slot_rank
    owner = jnp.full((slot_total,), entry_count, jnp.int32).at[slot_index].set(positions)
    filled = owner < entry_count
    source = jnp.minimum(owner, entry_count - 1)
    tile_of = entry_tile[source]
    kernel_of = jnp.where(filled, entry_kernel[source], 0)
    rows_ky = ky_bank[kernel_of] * filled[:, None, None].astype(ky_bank.dtype)
    pixels = jnp.concatenate([slice_tiles[tile_of], ctf_tiles[tile_of]], axis=2)
    outgoing = jnp.einsum(
        "syp,spc->syc", rows_ky, pixels, preferred_element_type=jnp.float32
    ).astype(jnp.bfloat16)
    incoming, kind_ids = (
        lax.all_to_all(outgoing, ("img", "pen"), split_axis=0, concat_axis=0, tiled=True),
        lax.all_to_all(kernel_of, ("img", "pen"), split_axis=0, concat_axis=0, tiled=True),
    )
    plane_start = lax.axis_index("pen") * planes
    z_columns = lax.dynamic_slice_in_dim(z_bank, plane_start, planes, 1)
    onehot = (kind_ids[:, None] == jnp.arange(NK, dtype=jnp.int32)[None, :]).astype(jnp.bfloat16)
    mixing = (onehot[:, :, None] * z_columns[None, :, :]).reshape(slot_total, NK * planes)
    per_kernel = jnp.dot(
        mixing.T, incoming.reshape(slot_total, -1), preferred_element_type=jnp.float32
    )
    brick_sums = apply_kx(per_kernel, kx_bank).reshape(rows_brick, 3, planes, KXH)
    denominator = brick_sums[:, 2] + 1.0
    grid_real = brick_sums[:, 0] / denominator
    grid_imag = brick_sums[:, 1] / denominator
    quarter = NBOX // 4
    row_x = lax.broadcasted_iota(jnp.int32, (2 * NBOX, 2 * KXH), 0)
    col_x = lax.broadcasted_iota(jnp.int32, (2 * NBOX, 2 * KXH), 1)
    kx_of = col_x % KXH
    phase_x = (row_x // 2) * kx_of + quarter * (col_x // KXH - row_x % 2)
    table_x = jnp.where(kx_of == 0, 1.0, 2.0) * jnp.cos(
        2.0 * math.pi / NBOX * (phase_x % NBOX).astype(jnp.float32)
    )
    row_y = lax.broadcasted_iota(jnp.int32, (2 * NBOX, 2 * NBOX), 0)
    col_y = lax.broadcasted_iota(jnp.int32, (2 * NBOX, 2 * NBOX), 1)
    phase_y = (row_y // 2) * (col_y // 2) + quarter * (col_y % 2 - row_y % 2)
    table_y = jnp.cos(2.0 * math.pi / NBOX * (phase_y % NBOX).astype(jnp.float32))
    norm_scale = 1.0 / math.sqrt(window * NBOX * KXH)
    row_z = lax.broadcasted_iota(jnp.int32, (2 * window, ZW), 0)
    col_z = lax.broadcasted_iota(jnp.int32, (2 * window, ZW), 1)
    phase_z = (row_z // 2) * col_z + quarter * (row_z % 2)
    table_z = norm_scale * jnp.cos(2.0 * math.pi / NBOX * (phase_z % NBOX).astype(jnp.float32))
    table_x, table_y, table_z = lax.optimization_barrier((table_x, table_y, table_z))
    contract_minor = (((1,), (1,)), ((), ()))
    stacked = (
        jnp.concatenate([grid_real, grid_imag], axis=2)
        .transpose(1, 0, 2)
        .reshape(planes * rows_brick, 2 * KXH)
    )
    after_x = lax.dot_general(
        table_x, stacked, contract_minor, precision=lax.Precision.HIGH
    ).reshape(img_count, -1, planes * rows_brick)
    block_in = lax.all_to_all(after_x, "img", split_axis=0, concat_axis=0, tiled=True)
    x_local = NBOX // img_count
    rows_y = (
        block_in.reshape(img_count, x_local, 2, planes, rows_brick)
        .transpose(3, 1, 0, 4, 2)
        .reshape(planes * x_local, 2 * NBOX)
    )
    after_y = lax.dot_general(
        table_y, rows_y, contract_minor, precision=lax.Precision.HIGH
    ).reshape(pen_count, -1, planes * x_local)
    block_z = lax.all_to_all(after_y, "pen", split_axis=0, concat_axis=0, tiled=True)
    y_local = NBOX // pen_count
    rows_z = (
        block_z.reshape(pen_count, y_local, 2, planes, x_local)
        .transpose(1, 4, 0, 3, 2)
        .reshape(y_local * x_local, 2 * window)
    )
    volume = jnp.dot(rows_z, table_z, precision=lax.Precision.HIGH)
    return volume.reshape(y_local, x_local, ZW)

def solution(mesh):
    return jax.shard_map(
        local,
        mesh=mesh,
        in_specs=(
            P(("img", "pen"), None, None),
            P(("img", "pen"), None, None),
            P(("img", "pen")),
            P(("img", "pen"), None),
            P(("img", "pen")),
            P(),
            P(),
            P(),
        ),
        out_specs=P("pen", "img", None),
        check_vma=False,
    )
```

profile of v0, /device:TPU:1, one launch (start us, length us, event | category | flops | bytes accessed | tf_op | source)
XLA Modules:
  0.0 445.7 jit_solution(8976628875556385993)
XLA Ops:
  0.0 1.0 convert_reduce_fusion
  1.7 1.0 scatter_custom_fusion
  2.7 1.9 gather_fusion
  4.6 0.8 all_to_all.15
  5.4 11.5 %all-to-all-start = ((s32[128,2,1]{1,2,0:T(1,128)}), s32[128,2,1]{1,2,0:T(1,128)S(1)}, u32[]{:S(2)}, u32[]{:S(2)}) async-start(s32[128,2,1]{1,2,0:T(1,128)} %bitcast.5), calls=%async_computation | async-start | bytes 131072 | tf_op jit(solution)/shard_map/all_to_all | solution.py:81
  16.9 1.9 gather_fusion.2
  18.8 11.7 %gather_fusion.3 = bf16[256,128,256]{2,1,0:T(8,128)(2,1)} fusion(bf16[64,128,256]{2,1,0:T(8,128)(2,1)} %param.8, s32[1024]{0:T(1024)S(1)} %pad_clamp_fusion), kind=kCustom, calls=%fused_computation.3 | custom fusion | bytes 33555456 | tf_op jit(solution)/shard_map/gather | solution.py:75
  30.5 8.4 %gather_fusion.4 = bf16[256,128,128]{2,1,0:T(8,128)(2,1)} fusion(bf16[64,128,128]{2,1,0:T(8,128)(2,1)S(1)} %copy-done, s32[1024]{0:T(1024)S(1)} %pad_clamp_fusion), kind=kCustom, calls=%fused_computation.4 | custom fusion | bytes 16778240 | tf_op jit(solution)/shard_map/gather | solution.py:75
  39.0 2.7 gather_fusion.1
  41.7 15.3 %fusion.7 = bf16[256,48,384]{2,1,0:T(8,128)(2,1)} fusion(bf16[256,128,128]{2,1,0:T(8,128)(2,1)} %gather_fusion.4, bf16[256,128,256]{2,1,0:T(8,128)(2,1)} %gather_fusion.3, bf16[256,48,128]{2,1,0:T(8,128)(2,1)} %gather_fusion.1, bf16[256]{0:T(256)(128)(2,1)S(1)} %fusion.52), kind=kOutput, calls=%fused_computation.16 | convolution fusion | flops 1264582656 | bytes 37749248 | tf_op jit(solution)/shard_map/syp,spc->syc/dot_general | solution.py:76
  57.0 10.8 %all-to-all-start.1 = ((bf16[256,48,384]{2,1,0:T(8,128)(2,1)}), bf16[256,48,384]{2,1,0:T(8,128)(2,1)}, u32[]{:S(2)}, u32[]{:S(2)}) async-start(bf16[256,48,384]{2,1,0:T(8,128)(2,1)} %fusion.7), calls=%async_computation.1 | async-start | bytes 18874368 | tf_op jit(solution)/shard_map/all_to_all | solution.py:80
  68.6 20.3 %fusion.15 = f32[1536,768]{1,0:T(8,128)} fusion(s32[1536]{0:T(1024)S(1)} %get-tuple-element.14, s32[1536]{0:T(1024)S(1)} %get-tuple-element.15, s32[768]{0:T(1024)S(1)} %get-tuple-element.19, s32[768]{0:T(1024)S(1)} %get-tuple-element.22, s32[1536]{0:T(1024)S(1)} %get-tuple-element.13, s32[1536]{0:T(1024)S(1)} %get-tuple-element.16, ...), kind=kLoop, calls=%fused_computation.24 | loop fusion | flops 22413312 | bytes 4760064 | tf_op jit(solution)/shard_map/mul | solution.py:99
  88.9 38.7 %fusion.6 = f32[1536,1536]{1,0:T(8,128)} fusion(s32[1536]{0:T(1024)S(1)} %get-tuple-element.14, s32[1536]{0:T(1024)S(1)} %get-tuple-element.15, s32[1536]{0:T(1024)S(1)} %get-tuple-element.13, s32[1536]{0:T(1024)S(1)} %get-tuple-element.16, pred[1536]{0:T(1024)(128)(4,1)S(1)} %get-tuple-element.17, pred[1536]{0:T(1024)(128)(4,1)S(1)} %get-tuple-element.18), kind=kLoop, calls=%fused_computation.13 | loop fusion | flops 37748736 | bytes 9464832 | tf_op jit(solution)/shard_map/cos | solution.py:105
  128.2 0.8 reduce.3
  129.3 48.4 %all-to-all-done.1 = bf16[256,48,384]{2,1,0:T(8,128)(2,1)} async-done(((bf16[256,48,384]{2,1,0:T(8,128)(2,1)}), bf16[256,48,384]{2,1,0:T(8,128)(2,1)}, u32[]{:S(2)}, u32[]{:S(2)}) %all-to-all-start.1) | async-done | bytes 9437216 | tf_op jit(solution)/shard_map/all_to_all | solution.py:80
  177.7 10.1 %copy.45 = bf16[32,8,48,384]{3,1,2,0:T(8,128)(2,1)} copy(bf16[32,8,48,384]{3,2,1,0:T(8,128)(2,1)} %bitcast.24) | data formatting | bytes 18874368
  187.8 11.5 %fusion.54.h_ref = f32[256,18432]{1,0:T(8,128)} fusion(bf16[256,256]{0,1:T(8,128)(2,1)S(1)} %bitcast.72, bf16[256,18432]{1,0:T(8,128)(2,1)} %bitcast.61), kind=kOutput, calls=%fused_computation.98 | convolution fusion | flops 2415919104 | bytes 28442624 | tf_op jit(solution)/shard_map/dot_general | solution.py:87
  199.3 22.3 %shard_map.82 = f32[2304,384]{1,0:T(8,128)} custom-call(f32[256,18432]{1,0:T(8,128)} %fusion.54.h_ref, bf16[16,128,384]{2,1,0:T(8,128)(2,1)} %w_ref.1), custom_call_target="tpu_custom_call" | custom-call | tf_op jit(solution)/shard_map/pallas_call | solution.py:44
  221.6 2.0 fusion.20
  223.6 0.8 copy-done.3
  224.8 1.4 copy.36
  226.6 5.9 %fusion.55 = f32[16,96,768]{2,1,0:T(8,128)S(1)} fusion(f32[16,96,768]{2,1,0:T(8,128)S(1)} %bitcast.69, f32[768,768,1]{1,0,2:T(8,128)S(1)} %bitcast.71), kind=kOutput, calls=%fused_computation.99 | convolution fusion | flops 5435817984 | bytes 11796480 | tf_op jit(solution)/shard_map/dot_general | solution.py:118
  232.6 65.7 %all_to_all.24 = f32[16,96,768]{2,1,0:T(8,128)} all-to-all(f32[16,96,768]{2,1,0:T(8,128)S(1)} %fusion.55), channel_id=1, replica_groups=mesh['img'=16,'pen'=8] {'img'}, dimensions={0} | all-to-all | bytes 9437184 | tf_op jit(solution)/shard_map/all_to_all | solution.py:121
  298.3 11.0 %reshape.113 = f32[16,48,2,16,48]{4,3,2,1,0:T(8,128)} reshape(f32[16,96,768]{2,1,0:T(8,128)} %all_to_all.24) | data formatting | bytes 9437184 | tf_op jit(solution)/shard_map/reshape | solution.py:124
  309.3 15.7 %copy.37 = f32[16,48,2,16,48]{1,3,2,4,0:T(8,128)} copy(f32[16,48,2,16,48]{4,3,2,1,0:T(8,128)} %reshape.113) | data formatting | bytes 9437184 | tf_op jit(solution)/shard_map/reshape | solution.py:124
  325.0 10.9 %reshape.114 = f32[768,1536]{0,1:T(8,128)} reshape(f32[16,48,16,48,2]{1,0,4,3,2:T(8,128)} %bitcast.62) | data formatting | bytes 9437184 | tf_op jit(solution)/shard_map/reshape | solution.py:126
  335.9 15.7 %fusion.16 = f32[8,192,768]{2,1,0:T(8,128)S(1)} fusion(f32[8,192,1536]{2,1,0:T(8,128)} %bitcast.70, f32[768,1536]{0,1:T(8,128)} %reshape.114), kind=kOutput, calls=%fused_computation.25 | convolution fusion | flops 10871635968 | bytes 18874368 | tf_op jit(solution)/shard_map/dot_general | solution.py:128
  351.6 58.6 %all_to_all.25 = f32[8,192,768]{2,1,0:T(8,128)} all-to-all(f32[8,192,768]{2,1,0:T(8,128)S(1)} %fusion.16), channel_id=1, replica_groups=mesh['img'=16,'pen'=8] {'pen'}, dimensions={0} | all-to-all | bytes 9437184 | tf_op jit(solution)/shard_map/all_to_all | solution.py:131
  410.2 11.0 %reshape.115 = f32[8,96,2,16,48]{4,3,2,1,0:T(8,128)} reshape(f32[8,192,768]{2,1,0:T(8,128)} %all_to_all.25) | data formatting | bytes 9437184 | tf_op jit(solution)/shard_map/reshape | solution.py:134
  421.2 11.8 %copy.39 = f32[96,48,8,16,2]{0,1,4,3,2:T(8,128)} copy(f32[96,48,8,16,2]{1,3,4,0,2:T(8,128)} %bitcast.63) | data formatting | bytes 9437184 | tf_op jit(solution)/shard_map/transpose | solution.py:135
  433.0 6.4 %copy.40 = f32[96,48,256]{2,1,0:T(8,128)} copy(f32[96,48,256]{0,1,2:T(8,128)} %bitcast.64) | data formatting | bytes 9437184 | tf_op jit(solution)/shard_map/dot_general | solution.py:138
  439.4 5.8 %fusion.28 = f32[96,48,128]{2,1,0:T(8,128)} fusion(f32[96,48,256]{2,1,0:T(8,128)} %copy.40, f32[256,128]{1,0:T(8,128)S(1)} %fusion.27), kind=kOutput, calls=%fused_computation.42 | convolution fusion | flops 905969664 | bytes 7208960 | tf_op jit(solution)/shard_map/dot_general | solution.py:138
  (41 shorter events, 3.2 us)
Async XLA Ops:
  0.0 30.5 %copy-start = (bf16[64,128,128]{2,1,0:T(8,128)(2,1)S(1)}, bf16[64,128,128]{2,1,0:T(8,128)(2,1)}, u32[]{:S(2)}) copy-start(bf16[64,128,128]{2,1,0:T(8,128)(2,1)} %param.9) | copy-start | bytes 6291460
  5.4 51.6 %all-to-all-start = ((s32[128,2,1]{1,2,0:T(1,128)}), s32[128,2,1]{1,2,0:T(1,128)S(1)}, u32[]{:S(2)}, u32[]{:S(2)}) async-start(s32[128,2,1]{1,2,0:T(1,128)} %bitcast.5), calls=%async_computation | async-start | bytes 131072 | tf_op jit(solution)/shard_map/all_to_all | solution.py:81
  30.5 8.5 %copy-start.2 = (bf16[16,48,128]{2,1,0:T(8,128)(2,1)S(1)}, bf16[16,48,128]{2,1,0:T(8,128)(2,1)}, u32[]{:S(2)}) copy-start(bf16[16,48,128]{2,1,0:T(8,128)(2,1)} %param.13) | copy-start | bytes 589828
  57.0 120.7 %all-to-all-start.1 = ((bf16[256,48,384]{2,1,0:T(8,128)(2,1)}), bf16[256,48,384]{2,1,0:T(8,128)(2,1)}, u32[]{:S(2)}, u32[]{:S(2)}) async-start(bf16[256,48,384]{2,1,0:T(8,128)(2,1)} %fusion.7), calls=%async_computation.1 | async-start | bytes 18874368 | tf_op jit(solution)/shard_map/all_to_all | solution.py:80
  88.9 38.7 %copy-start.4 = (bf16[16,128]{1,0:T(8,128)(2,1)S(1)}, bf16[16,128]{1,0:T(8,128)(2,1)}, u32[]{:S(2)}) copy-start(bf16[16,128]{1,0:T(8,128)(2,1)} %param.15) | copy-start | bytes 12292
  221.6 2.7 copy-start.3
  224.3 2.2 slice-start
  224.5 2.2 slice-start.1
  433.0 12.2 %copy-start.1 = (bf16[64,128,128]{2,1,0:T(8,128)(2,1)S(1)}, bf16[64,128,128]{2,1,0:T(8,128)(2,1)}, u32[]{:S(2)}) copy-start(bf16[64,128,128]{2,1,0:T(8,128)(2,1)} %param.9) | copy-start | bytes 6291460
where the time goes:
time: 455 us; the launch traced here: 446 us
  blocking collectives  124 us (27%)
  local copies, waits for them, and re-layouts  109 us (24%)
  other arithmetic  64.7 us (14%)
  matrix products  54.1 us (12%)
  waiting for transfers between devices  48.4 us (11%)
  starting transfers between devices  22.3 us (5%)
  Pallas kernels  22.3 us (5%)
    all_to_all x1, blocking collectives, local(): lax.all_to_all(after_x, 'img', split_axis=0, concat_axis=0, tiled=True)  65.7 us
    all_to_all x1, blocking collectives, local(): lax.all_to_all(after_y, 'pen', split_axis=0, concat_axis=0, tiled=True)  58.6 us
    all_to_all x1, waiting for transfers between devices, local(): lax.all_to_all(outgoing, ('img', 'pen'), split_axis=0, concat_axis=0, til...  48.4 us
    cos x1, other arithmetic, local(): jnp.cos(2.0 * math.pi / NBOX * (phase_y % NBOX).astype(jnp.float32))  38.7 us
    reshape x2, local copies, waits for them, and re-layouts, local(): block_in.reshape(img_count, x_local, 2, planes, rows_brick)  26.8 us
    pallas_call x1, Pallas kernels, apply_kx(): pl.pallas_call(kx_kernel, grid=(kernels,), in_specs=[pl.BlockSpec((planes...  22.3 us
    mul x1, other arithmetic, local(): jnp.where(kx_of == 0, 1.0, 2.0)  20.3 us
    gather x2, local copies, waits for them, and re-layouts, local(): pixels = jnp.concatenate([slice_tiles[tile_of], ctf_tiles[tile_of]], axis=2)  20.2 us
  transfers between devices with their start and end apart: 2, of which 1 were waited for; matrix products, arithmetic and copies ran while one was open for 23% of the time, Pallas kernels for 0%

commit v1 on v0

--- a/solution.py
+++ b/solution.py
@@ -24,32 +24,32 @@
     def _():
         o_ref[...] = jnp.zeros(o_ref.shape, o_ref.dtype)
 
+    rows, planes, _ = h_ref.shape
     pix = w_ref.shape[1]
-    h = jnp.concatenate(
-        [h_ref[:, m * pix:(m + 1) * pix] for m in range(h_ref.shape[1] // pix)], axis=0
-    )
-    hi = h.astype(jnp.bfloat16)
-    lo = (h - hi.astype(jnp.float32)).astype(jnp.bfloat16)
     w = w_ref[0]
-    o_ref[...] += jnp.dot(hi, w, preferred_element_type=jnp.float32) + jnp.dot(
-        lo, w, preferred_element_type=jnp.float32
-    )
+    for channel in range(o_ref.shape[0]):
+        h = h_ref[:, :, channel * pix:(channel + 1) * pix].reshape(rows * planes, pix)
+        hi = h.astype(jnp.bfloat16)
+        lo = (h - hi.astype(jnp.float32)).astype(jnp.bfloat16)
+        o_ref[channel] += jnp.dot(hi, w, preferred_element_type=jnp.float32) + jnp.dot(
+            lo, w, preferred_element_type=jnp.float32
+        )
 
 
 def apply_kx(per_kernel, kx_bank):
     kernels, pix, cols = kx_bank.shape
-    planes = per_kernel.shape[0] // kernels
-    width = per_kernel.shape[1]
-    rows = planes * width // pix
+    planes = per_kernel.shape[1] // kernels
+    rows, width = per_kernel.shape[0], per_kernel.shape[2]
+    channels = width // pix
     return pl.pallas_call(
         kx_kernel,
         grid=(kernels,),
         in_specs=[
-            pl.BlockSpec((planes, width), lambda k: (k, 0)),
+            pl.BlockSpec((rows, planes, width), lambda k: (0, k, 0)),
             pl.BlockSpec((1, pix, cols), lambda k: (k, 0, 0)),
         ],
-        out_specs=pl.BlockSpec((rows, cols), lambda k: (0, 0)),
-        out_shape=jax.ShapeDtypeStruct((rows, cols), jnp.float32),
+        out_specs=pl.BlockSpec((channels, planes * rows, cols), lambda k: (0, 0, 0)),
+        out_shape=jax.ShapeDtypeStruct((channels, planes * rows, cols), jnp.float32),
     )(per_kernel, kx_bank)
 
 def local(slice_tiles, ctf_tiles, entry_tile, entry_brick, entry_kernel, ky_bank, kx_bank, z_bank):
@@ -84,13 +84,13 @@
     z_columns = lax.dynamic_slice_in_dim(z_bank, plane_start, planes, 1)
     onehot = (kind_ids[:, None] == jnp.arange(NK, dtype=jnp.int32)[None, :]).astype(jnp.bfloat16)
     mixing = (onehot[:, :, None] * z_columns[None, :, :]).reshape(slot_total, NK * planes)
-    per_kernel = jnp.dot(
-        mixing.T, incoming.reshape(slot_total, -1), preferred_element_type=jnp.float32
-    )
-    brick_sums = apply_kx(per_kernel, kx_bank).reshape(rows_brick, 3, planes, KXH)
-    denominator = brick_sums[:, 2] + 1.0
-    grid_real = brick_sums[:, 0] / denominator
-    grid_imag = brick_sums[:, 1] / denominator
+    per_kernel = lax.dot_general(
+        mixing, incoming, (((0,), (0,)), ((), ())), preferred_element_type=jnp.float32
+    ).transpose(1, 0, 2)
+    brick_sums = apply_kx(per_kernel, kx_bank)
+    denominator = brick_sums[2] + 1.0
+    grid_real = brick_sums[0] / denominator
+    grid_imag = brick_sums[1] / denominator
     quarter = NBOX // 4
     row_x = lax.broadcasted_iota(jnp.int32, (2 * NBOX, 2 * KXH), 0)
     col_x = lax.broadcasted_iota(jnp.int32, (2 * NBOX, 2 * KXH), 1)
@@ -111,7 +111,8 @@
     table_x, table_y, table_z = lax.optimization_barrier((table_x, table_y, table_z))
     contract_minor = (((1,), (1,)), ((), ()))
     stacked = (
-        jnp.concatenate([grid_real, grid_imag], axis=2)
+        jnp.concatenate([grid_real, grid_imag], axis=1)
+        .reshape(rows_brick, planes, 2 * KXH)
         .transpose(1, 0, 2)
         .reshape(planes * rows_brick, 2 * KXH)
     )

time: 455 us -> 445 us (0.978)
  local copies, waits for them, and re-layouts: 109 us -> 97.5 us
    unnamed x15 -> x12, local copies, waits for them, and re-layouts: 11.4 us -> 0.02 us
where the time goes in v1:
time: 445 us; the launch traced here: 437 us
  blocking collectives  124 us (28%)
  local copies, waits for them, and re-layouts  97.5 us (22%)
  other arithmetic  65 us (15%)
  matrix products  56 us (13%)
  waiting for transfers between devices  48.3 us (11%)
  starting transfers between devices  22.4 us (5%)
  Pallas kernels  22.3 us (5%)
    all_to_all x1, blocking collectives, local(): lax.all_to_all(after_x, 'img', split_axis=0, concat_axis=0, tiled=True)  66 us
    all_to_all x1, blocking collectives, local(): lax.all_to_all(after_y, 'pen', split_axis=0, concat_axis=0, tiled=True)  58.5 us
    all_to_all x1, waiting for transfers between devices, local(): lax.all_to_all(outgoing, ('img', 'pen'), split_axis=0, concat_axis=0, til...  48.3 us
    cos x1, other arithmetic, local(): jnp.cos(2.0 * math.pi / NBOX * (phase_y % NBOX).astype(jnp.float32))  38.7 us
    reshape x2, local copies, waits for them, and re-layouts, local(): block_in.reshape(img_count, x_local, 2, planes, rows_brick)  26.8 us
    pallas_call x1, Pallas kernels, apply_kx(): pl.pallas_call(kx_kernel, grid=(kernels,), in_specs=[pl.BlockSpec((rows,...  22.3 us
    mul x1, other arithmetic, local(): jnp.where(kx_of == 0, 1.0, 2.0)  20.3 us
    gather x2, local copies, waits for them, and re-layouts, local(): pixels = jnp.concatenate([slice_tiles[tile_of], ctf_tiles[tile_of]], axis=2)  20.2 us
  transfers between devices with their start and end apart: 2, of which 1 were waited for; matrix products, arithmetic and copies ran while one was open for 23% of the time, Pallas kernels for 0%

profile of v1, /device:TPU:1, one launch (start us, length us, event | category | flops | bytes accessed | tf_op | source)
XLA Modules:
  0.0 436.5 jit_solution(15517947641466990358)
XLA Ops:
  0.0 1.0 convert_reduce_fusion
  1.0 0.7 fusion.51
  1.7 1.0 scatter_custom_fusion
  2.7 1.9 gather_fusion
  4.6 0.8 all_to_all.15
  5.4 11.5 %all-to-all-start = ((s32[128,2,1]{1,2,0:T(1,128)}), s32[128,2,1]{1,2,0:T(1,128)S(1)}, u32[]{:S(2)}, u32[]{:S(2)}) async-start(s32[128,2,1]{1,2,0:T(1,128)} %bitcast.5), calls=%async_computation | async-start | bytes 131072 | tf_op jit(solution)/shard_map/all_to_all | solution.py:81
  16.9 1.9 gather_fusion.2
  18.8 11.7 %gather_fusion.3 = bf16[256,128,256]{2,1,0:T(8,128)(2,1)} fusion(bf16[64,128,256]{2,1,0:T(8,128)(2,1)} %param.8, s32[1024]{0:T(1024)S(1)} %pad_clamp_fusion), kind=kCustom, calls=%fused_computation.3 | custom fusion | bytes 33555456 | tf_op jit(solution)/shard_map/gather | solution.py:75
  30.5 8.4 %gather_fusion.4 = bf16[256,128,128]{2,1,0:T(8,128)(2,1)} fusion(bf16[64,128,128]{2,1,0:T(8,128)(2,1)S(1)} %copy-done, s32[1024]{0:T(1024)S(1)} %pad_clamp_fusion), kind=kCustom, calls=%fused_computation.4 | custom fusion | bytes 16778240 | tf_op jit(solution)/shard_map/gather | solution.py:75
  39.0 2.7 gather_fusion.1
  41.7 15.3 %fusion.12 = bf16[256,48,384]{2,1,0:T(8,128)(2,1)} fusion(bf16[256,128,128]{2,1,0:T(8,128)(2,1)} %gather_fusion.4, bf16[256,128,256]{2,1,0:T(8,128)(2,1)} %gather_fusion.3, bf16[256,48,128]{2,1,0:T(8,128)(2,1)} %gather_fusion.1, bf16[256]{0:T(256)(128)(2,1)S(1)} %fusion.54), kind=kOutput, calls=%fused_computation.19 | convolution fusion | flops 1264582656 | bytes 37749248 | tf_op jit(solution)/shard_map/syp,spc->syc/dot_general | solution.py:76
  56.9 10.9 %all-to-all-start.1 = ((bf16[256,48,384]{2,1,0:T(8,128)(2,1)}), bf16[256,48,384]{2,1,0:T(8,128)(2,1)}, u32[]{:S(2)}, u32[]{:S(2)}) async-start(bf16[256,48,384]{2,1,0:T(8,128)(2,1)} %fusion.12), calls=%async_computation.1 | async-start | bytes 18874368 | tf_op jit(solution)/shard_map/all_to_all | solution.py:80
  68.1 0.6 fusion.28
  68.8 20.3 %fusion.20 = f32[1536,768]{1,0:T(8,128)} fusion(s32[1536]{0:T(1024)S(1)} %get-tuple-element.16, s32[1536]{0:T(1024)S(1)} %get-tuple-element.17, s32[768]{0:T(1024)S(1)} %get-tuple-element.21, s32[768]{0:T(1024)S(1)} %get-tuple-element.24, s32[1536]{0:T(1024)S(1)} %get-tuple-element.15, s32[1536]{0:T(1024)S(1)} %get-tuple-element.18, ...), kind=kLoop, calls=%fused_computation.27 | loop fusion | flops 22413312 | bytes 4760064 | tf_op jit(solution)/shard_map/mul | solution.py:99
  89.1 38.7 %fusion.6 = f32[1536,1536]{1,0:T(8,128)} fusion(s32[1536]{0:T(1024)S(1)} %get-tuple-element.16, s32[1536]{0:T(1024)S(1)} %get-tuple-element.17, s32[1536]{0:T(1024)S(1)} %get-tuple-element.15, s32[1536]{0:T(1024)S(1)} %get-tuple-element.18, pred[1536]{0:T(1024)(128)(4,1)S(1)} %get-tuple-element.19, pred[1536]{0:T(1024)(128)(4,1)S(1)} %get-tuple-element.20), kind=kLoop, calls=%fused_computation.13 | loop fusion | flops 37748736 | bytes 9464832 | tf_op jit(solution)/shard_map/cos | solution.py:105
  128.3 0.8 reduce.3
  129.4 48.3 %all-to-all-done.1 = bf16[256,48,384]{2,1,0:T(8,128)(2,1)} async-done(((bf16[256,48,384]{2,1,0:T(8,128)(2,1)}), bf16[256,48,384]{2,1,0:T(8,128)(2,1)}, u32[]{:S(2)}, u32[]{:S(2)}) %all-to-all-start.1) | async-done | bytes 9437216 | tf_op jit(solution)/shard_map/all_to_all | solution.py:80
  177.7 13.4 %fusion.9.h_ref = f32[48,256,384]{2,1,0:T(8,128)} fusion(bf16[256,48,384]{2,1,0:T(8,128)(2,1)} %all-to-all-done.1, bf16[256,256]{0,1:T(8,128)(2,1)S(1)} %bitcast_multiply_fusion), kind=kOutput, calls=%fused_computation.17 | convolution fusion | flops 2415919104 | bytes 28442624 | tf_op jit(solution)/shard_map/dot_general | solution.py:87
  191.1 22.3 %shard_map.82 = f32[3,768,384]{2,1,0:T(8,128)} custom-call(f32[48,256,384]{2,1,0:T(8,128)} %fusion.9.h_ref, bf16[16,128,384]{2,1,0:T(8,128)(2,1)} %w_ref.1), custom_call_target="tpu_custom_call" | custom-call | tf_op jit(solution)/shard_map/pallas_call | solution.py:44
  213.5 2.3 slice_divide_fusion.1
  216.1 1.4 copy.26
  217.5 5.9 %fusion.56 = f32[16,96,768]{2,1,0:T(8,128)S(1)} fusion(f32[16,96,768]{2,1,0:T(8,128)S(1)} %bitcast.49, f32[768,768,1]{1,0,2:T(8,128)S(1)} %bitcast.51), kind=kOutput, calls=%fused_computation.98 | convolution fusion | flops 5435817984 | bytes 11796480 | tf_op jit(solution)/shard_map/dot_general | solution.py:119
  223.4 66.0 %all_to_all.24 = f32[16,96,768]{2,1,0:T(8,128)} all-to-all(f32[16,96,768]{2,1,0:T(8,128)S(1)} %fusion.56), channel_id=1, replica_groups=mesh['img'=16,'pen'=8] {'img'}, dimensions={0} | all-to-all | bytes 9437184 | tf_op jit(solution)/shard_map/all_to_all | solution.py:122
  289.4 11.0 %reshape.82 = f32[16,48,2,16,48]{4,3,2,1,0:T(8,128)} reshape(f32[16,96,768]{2,1,0:T(8,128)} %all_to_all.24) | data formatting | bytes 9437184 | tf_op jit(solution)/shard_map/reshape | solution.py:125
  300.4 15.7 %copy.27 = f32[16,48,2,16,48]{1,3,2,4,0:T(8,128)} copy(f32[16,48,2,16,48]{4,3,2,1,0:T(8,128)} %reshape.82) | data formatting | bytes 9437184 | tf_op jit(solution)/shard_map/reshape | solution.py:125
  316.2 10.9 %reshape.83 = f32[768,1536]{0,1:T(8,128)} reshape(f32[16,48,16,48,2]{1,0,4,3,2:T(8,128)} %bitcast.44) | data formatting | bytes 9437184 | tf_op jit(solution)/shard_map/reshape | solution.py:127
  327.1 15.7 %fusion.21 = f32[8,192,768]{2,1,0:T(8,128)S(1)} fusion(f32[8,192,1536]{2,1,0:T(8,128)} %bitcast.50, f32[768,1536]{0,1:T(8,128)} %reshape.83), kind=kOutput, calls=%fused_computation.28 | convolution fusion | flops 10871635968 | bytes 18874368 | tf_op jit(solution)/shard_map/dot_general | solution.py:129
  342.8 58.5 %all_to_all.25 = f32[8,192,768]{2,1,0:T(8,128)} all-to-all(f32[8,192,768]{2,1,0:T(8,128)S(1)} %fusion.21), channel_id=1, replica_groups=mesh['img'=16,'pen'=8] {'pen'}, dimensions={0} | all-to-all | bytes 9437184 | tf_op jit(solution)/shard_map/all_to_all | solution.py:132
  401.2 11.0 %reshape.84 = f32[8,96,2,16,48]{4,3,2,1,0:T(8,128)} reshape(f32[8,192,768]{2,1,0:T(8,128)} %all_to_all.25) | data formatting | bytes 9437184 | tf_op jit(solution)/shard_map/reshape | solution.py:135
  412.3 11.8 %copy.29 = f32[96,48,8,16,2]{0,1,4,3,2:T(8,128)} copy(f32[96,48,8,16,2]{1,3,4,0,2:T(8,128)} %bitcast.45) | data formatting | bytes 9437184 | tf_op jit(solution)/shard_map/transpose | solution.py:136
  424.1 6.4 %copy.30 = f32[96,48,256]{2,1,0:T(8,128)} copy(f32[96,48,256]{0,1,2:T(8,128)} %bitcast.46) | data formatting | bytes 9437184 | tf_op jit(solution)/shard_map/dot_general | solution.py:139
  430.5 5.8 %fusion.29 = f32[96,48,128]{2,1,0:T(8,128)} fusion(f32[96,48,256]{2,1,0:T(8,128)} %copy.30, f32[256,128]{1,0:T(8,128)S(1)} %fusion.28), kind=kOutput, calls=%fused_computation.41 | convolution fusion | flops 905969664 | bytes 7208960 | tf_op jit(solution)/shard_map/dot_general | solution.py:139
  (38 shorter events, 1.3 us)
Async XLA Ops:
  0.0 30.5 %copy-start = (bf16[64,128,128]{2,1,0:T(8,128)(2,1)S(1)}, bf16[64,128,128]{2,1,0:T(8,128)(2,1)}, u32[]{:S(2)}) copy-start(bf16[64,128,128]{2,1,0:T(8,128)(2,1)} %param.9) | copy-start | bytes 6291460
  5.4 51.6 %all-to-all-start = ((s32[128,2,1]{1,2,0:T(1,128)}), s32[128,2,1]{1,2,0:T(1,128)S(1)}, u32[]{:S(2)}, u32[]{:S(2)}) async-start(s32[128,2,1]{1,2,0:T(1,128)} %bitcast.5), calls=%async_computation | async-start | bytes 131072 | tf_op jit(solution)/shard_map/all_to_all | solution.py:81
  30.5 8.4 %copy-start.2 = (bf16[16,48,128]{2,1,0:T(8,128)(2,1)S(1)}, bf16[16,48,128]{2,1,0:T(8,128)(2,1)}, u32[]{:S(2)}) copy-start(bf16[16,48,128]{2,1,0:T(8,128)(2,1)} %param.13) | copy-start | bytes 589828
  56.9 10.9 %copy-start.3 = (bf16[16,128]{1,0:T(8,128)(2,1)S(1)}, bf16[16,128]{1,0:T(8,128)(2,1)}, u32[]{:S(2)}) copy-start(bf16[16,128]{1,0:T(8,128)(2,1)} %param.15) | copy-start | bytes 12292
  56.9 120.8 %all-to-all-start.1 = ((bf16[256,48,384]{2,1,0:T(8,128)(2,1)}), bf16[256,48,384]{2,1,0:T(8,128)(2,1)}, u32[]{:S(2)}, u32[]{:S(2)}) async-start(bf16[256,48,384]{2,1,0:T(8,128)(2,1)} %fusion.12), calls=%async_computation.1 | async-start | bytes 18874368 | tf_op jit(solution)/shard_map/all_to_all | solution.py:80
  213.5 4.0 slice-start
  215.8 1.7 slice-start.1
  424.1 12.2 %copy-start.1 = (bf16[64,128,128]{2,1,0:T(8,128)(2,1)S(1)}, bf16[64,128,128]{2,1,0:T(8,128)(2,1)}, u32[]{:S(2)}) copy-start(bf16[64,128,128]{2,1,0:T(8,128)(2,1)} %param.9) | copy-start | bytes 6291460
